TPU v7x, 256 devices: a whole 4x4x8 slice. The times are simulated.
256 devices in a mesh: patch: 32 (over y, z), req: 4 (over x), owner: 2 (over core).
Axes of the slice: x: 4, y: 4, z: 8, core: 2. Of those that a mesh axis runs over, the one named last changes fastest.
Arguments:
- latents: bfloat16 [8, 256, 256, 320], P('req', 'patch', 'owner'), may hold values from -24 to 24
- timestep_embedding: bfloat16 [8, 1280], P('req'), may hold values from -6 to 6
- embedding_weight: bfloat16 [1280, 320], replicated, may hold values from -0.15625 to 0.15625
- group_norm_gain: float32 [2, 320], replicated, may hold values from 0.25 to 1.75
- group_norm_shift: float32 [2, 320], replicated, may hold values from -3 to 3
- kernel_weight: bfloat16 [2, 9, 320, 320], replicated, may hold values from -0.109375 to 0.109375
- plugin_reduce_library: bfloat16 [8, 2, 184320], P(('req', 'owner'), None, 'patch'), may hold values from -0.109375 to 0.109375
- plugin_expand_library: bfloat16 [8, 2, 20480], P(('req', 'owner'), None, 'patch'), may hold values from -0.75 to 0.75
- image_adapter: int32 [8, 1], P('req'), may hold values from 0 to 7
- adapter_bank_row: int32 [8], replicated, may hold values from 0 to 7, each once
Outputs:
- result: bfloat16 [8, 256, 256, 320], P('req', 'patch', 'owner')
Inputs may be any that keep to these rules, and one draw needn't show every extreme that they name: `image_adapter`: each image names one adapter; every adapter is named by some image. A permutation: adapter a is stored in bank row adapter_bank_row[a].
All inputs are finite; a program needn't handle non-finite values.
Results may differ from a plain program's by a relative error of at most 0.0055.
Values may be sent and summed in bfloat16 or wider, within the bound.
A program may use at most 128 MiB of HBM per device.

v0:
```python
import jax
import jax.numpy as jnp
from jax import lax
from jax.sharding import PartitionSpec as P

GROUPS = 32


def padded_2(block, sides, width):
    for axis, dim in sides:
        count = lax.axis_size(axis)
        forward = [(i, i + 1) for i in range(count - 1)]
        backward = [(target, source) for source, target in forward]
        low = lax.ppermute(
            lax.slice_in_dim(block, block.shape[dim] - width, None, axis=dim), axis, forward
        )
        high = lax.ppermute(lax.slice_in_dim(block, 0, width, axis=dim), axis, backward)
        block = jnp.concatenate([low, block, high], axis=dim)
    return block


def group_act(values, gain, shift):
    images, rows, columns, chans = values.shape
    grouped = values.reshape(images, rows, columns, GROUPS, chans // GROUPS)
    count = rows * columns * (chans // GROUPS) * lax.axis_size("patch") * lax.axis_size("owner")
    total = lax.psum(jnp.sum(grouped, axis=(1, 2, 4)), ("patch", "owner"))
    mean = total / count
    centered = grouped - mean[:, None, None, :, None]
    spread = lax.psum(jnp.sum(centered * centered, axis=(1, 2, 4)), ("patch", "owner"))
    var = spread / count
    normed = (centered / jnp.sqrt(var + 1e-05)[:, None, None, :, None]).reshape(values.shape)
    return jax.nn.silu(normed * gain + shift).astype(jnp.bfloat16)


def block_conv(act, kernel, reducing_filter, expanding_linear_map):
    images, rows, columns, chans = act.shape
    outward = kernel.shape[2]
    padded = padded_2(act, (("patch", 1), ("owner", 2)), 1)
    joined = jnp.concatenate(
        [jnp.broadcast_to(kernel[None], (images,) + kernel.shape), reducing_filter], axis=3
    )
    accum = jnp.zeros((images, rows, columns, joined.shape[3]), jnp.float32)
    for tap in range(9):
        row_off, col_off = divmod(tap, 3)
        window = padded[:, row_off : row_off + rows, col_off : col_off + columns, :]
        accum = accum + jnp.einsum(
            "bhwc,bcd->bhwd", window, joined[:, tap], preferred_element_type=jnp.float32
        )
    lowpart = accum[..., outward:].astype(jnp.bfloat16)
    return accum[..., :outward] + jnp.einsum(
        "bhwr,brd->bhwd", lowpart, expanding_linear_map, preferred_element_type=jnp.float32
    )


def local(
    latents,
    timestep_embedding,
    embedding_weight,
    group_norm_gain,
    group_norm_shift,
    kernel_weight,
    plugin_reduce_library,
    plugin_expand_library,
    image_adapter,
    adapter_bank_row,
):
    images, rows, columns, chans = latents.shape
    wanted = image_adapter[:, 0]
    table = jnp.arange(adapter_bank_row.shape[0], dtype=jnp.int32)
    slots = jnp.sum(
        jnp.where(wanted[:, None] == table[None, :], adapter_bank_row[None, :], 0), axis=1
    )
    full_down, full_up = (
        lax.all_gather(plugin_reduce_library, "patch", axis=2, tiled=True),
        lax.all_gather(plugin_expand_library, "patch", axis=2, tiled=True),
    )
    pieces = (
        lax.all_gather(full_down, ("req", "owner"), axis=0, tiled=True),
        lax.all_gather(full_up, ("req", "owner"), axis=0, tiled=True),
    )
    count = pieces[0].shape[0]
    match = (slots[:, None] == jnp.arange(count, dtype=jnp.int32)[None, :]).astype(jnp.bfloat16)
    first = jnp.einsum("ik,kjs->ijs", match, pieces[0], preferred_element_type=jnp.float32)
    second = jnp.einsum("ik,kjs->ijs", match, pieces[1], preferred_element_type=jnp.float32)
    down_sel = first.astype(jnp.bfloat16)
    up_sel = second.astype(jnp.bfloat16)
    rank = up_sel.shape[2] // chans
    down_all = down_sel.reshape(images, 2, 9, chans, rank)
    up_all = up_sel.reshape(images, 2, rank, chans)
    temb = jax.nn.silu(timestep_embedding.astype(jnp.float32)).astype(jnp.bfloat16)
    proj = jnp.dot(temb, embedding_weight, preferred_element_type=jnp.float32)
    source = latents.astype(jnp.float32)
    act1 = group_act(source, group_norm_gain[0], group_norm_shift[0])
    hidden1 = (
        block_conv(act1, kernel_weight[0], down_all[:, 0], up_all[:, 0]) + proj[:, None, None, :]
    ).astype(jnp.bfloat16)
    act2 = group_act(hidden1.astype(jnp.float32), group_norm_gain[1], group_norm_shift[1])
    result = source + block_conv(act2, kernel_weight[1], down_all[:, 1], up_all[:, 1])
    return result.astype(jnp.bfloat16)


def solution(mesh):
    in_specs = (
        P("req", "patch", "owner", None),
        P("req", None),
        P(),
        P(),
        P(),
        P(),
        P(("req", "owner"), None, "patch"),
        P(("req", "owner"), None, "patch"),
        P("req", None),
        P(),
    )
    out_specs = P("req", "patch", "owner", None)
    return jax.shard_map(local, mesh=mesh, in_specs=in_specs, out_specs=out_specs, check_vma=False)
```

profile of v0, /device:TPU:1, one launch (start us, length us, event | category | flops | bytes accessed | tf_op | source)
XLA Modules:
  0.0 778.4 jit_solution(10491722644223189108)
XLA Ops:
  6.6 47.2 %all_gather.12 = bf16[1,2,184320]{2,1,0:T(2,128)(2,1)} all-gather(bf16[1,2,5760]{2,1,0:T(2,128)(2,1)} %param.16), channel_id=1, replica_groups=mesh['patch'=32,'req'=4,'owner'=2] {'patch'}, dimensions={2}, use_global_device_ids=true | all-gather | bytes 760320 | tf_op jit(solution)/shard_map/all_gather | solution.py:74
  55.6 135.6 %psum.28 = f32[2,32]{1,0:T(2,128)S(1)} all-reduce(f32[2,32]{1,0:T(2,128)S(1)} %reduce_sum.59), channel_id=1, replica_groups=mesh['patch'=32,'req'=4,'owner'=2] {'patch','owner'}, use_global_device_ids=true, to_apply=%region_2.3 | all-reduce | flops 64 | bytes 512 | tf_op jit(solution)/shard_map/psum | solution.py:26
  192.2 124.0 %psum.29 = f32[2,32]{1,0:T(2,128)S(1)} all-reduce(f32[2,32]{1,0:T(2,128)S(1)} %reduce_sum.62), channel_id=1, replica_groups=mesh['patch'=32,'req'=4,'owner'=2] {'patch','owner'}, use_global_device_ids=true, to_apply=%region_5.6 | all-reduce | flops 64 | bytes 512 | tf_op jit(solution)/shard_map/psum | solution.py:29
  320.5 32.0 %all_gather.14 = bf16[1,2,20480]{2,1,0:T(2,128)(2,1)S(1)} all-gather(bf16[1,2,640]{2,1,0:T(2,128)(2,1)S(1)} %copy-done.16), channel_id=1, replica_groups=mesh['patch'=32,'req'=4,'owner'=2] {'patch'}, dimensions={2}, use_global_device_ids=true | all-gather | bytes 84480 | tf_op jit(solution)/shard_map/all_gather | solution.py:75
  352.5 24.4 %all_gather.15 = bf16[8,2,20480]{2,1,0:T(2,128)(2,1)S(1)} all-gather(bf16[1,2,20480]{2,1,0:T(2,128)(2,1)S(1)} %all_gather.14), channel_id=1, replica_groups=mesh['patch'=32,'req'=4,'owner'=2] {'req','owner'}, dimensions={0}, use_global_device_ids=true | all-gather | bytes 737280 | tf_op jit(solution)/shard_map/all_gather | solution.py:79
  377.0 4.8 slice_bitcast_fusion
  390.1 3.5 collective-permute-start.3
  398.0 5.7 pad_maximum_fusion
  403.7 10.7 %convolution_convert_fusion = bf16[2,2,184320]{2,0,1:T(2,128)(2,1)} fusion(bf16[8,2,184320]{2,1,0:T(2,128)(2,1)} %all-gather.2.cloned.1.call-done, s32[2]{0:T(128)S(1)} %fusion.123), kind=kOutput, calls=%fused_computation | convolution fusion | flops 12533776 | bytes 7372808 | tf_op jit(solution)/shard_map/ik,kjs->ijs/dot_general | solution.py:83
  414.4 4.7 reshape.54
  419.1 3.3 fusion.145
  425.4 2.7 fusion.52
  428.2 2.9 fusion.54
  431.1 2.9 fusion.50
  434.0 2.7 fusion.48
  436.7 2.7 fusion.80
  439.4 2.7 fusion.14
  442.2 2.7 fusion.18
  444.9 9.6 %add_add_fusion.1 = f32[2,8,128,384]{2,3,1,0:T(8,128)} fusion(f32[2,8,128,384]{2,3,1,0:T(8,128)} %fusion.18, f32[2,8,128,384]{2,3,1,0:T(8,128)} %fusion.48, f32[2,8,128,384]{2,3,1,0:T(8,128)} %fusion.50, f32[2,8,128,384]{2,3,1,0:T(8,128)} %fusion.80, f32[2,8,128,384]{2,3,1,0:T(8,128)S(1)} %copy-done.10, f32[2,8,128,384]{2,3,1,0:T(8,128)} %fusion.54, ...), kind=kOutput, calls=%fused_computation.45 | convolution fusion | flops 510590976 | bytes 35520512 | tf_op jit(solution)/shard_map/bhwc,bcd->bhwd/dot_general | solution.py:46
  457.3 122.8 %psum.30 = f32[2,32]{1,0:T(2,128)S(1)} all-reduce(f32[2,32]{1,0:T(2,128)S(1)} %reduce_sum.82), channel_id=1, replica_groups=mesh['patch'=32,'req'=4,'owner'=2] {'patch','owner'}, use_global_device_ids=true, to_apply=%region_9.10 | all-reduce | flops 64 | bytes 512 | tf_op jit(solution)/shard_map/psum | solution.py:26
  581.0 127.5 %psum.31 = f32[2,32]{1,0:T(2,128)S(1)} all-reduce(f32[2,32]{1,0:T(2,128)S(1)} %reduce_sum.85), channel_id=1, replica_groups=mesh['patch'=32,'req'=4,'owner'=2] {'patch','owner'}, use_global_device_ids=true, to_apply=%region_12.13 | all-reduce | flops 64 | bytes 512 | tf_op jit(solution)/shard_map/psum | solution.py:29
  714.9 3.2 fusion.97
  727.7 3.7 collective-permute-start.7
  731.4 4.1 fusion.22
  735.5 2.7 fusion.26
  741.8 5.0 pad_maximum_fusion.1
  746.8 2.7 fusion.42
  749.5 2.7 fusion.38
  752.2 2.9 fusion.40
  755.1 2.9 fusion.36
  758.0 2.7 fusion.34
  760.7 8.9 %add_add_fusion = f32[2,8,128,384]{2,3,1,0:T(8,128)S(1)} fusion(f32[2,8,128,384]{2,3,1,0:T(8,128)} %fusion.26, f32[2,8,128,384]{2,3,1,0:T(8,128)} %fusion.34, f32[2,8,128,384]{2,3,1,0:T(8,128)} %fusion.36, f32[2,8,128,384]{2,3,1,0:T(8,128)S(1)} %copy-done.9, f32[2,8,128,384]{2,3,1,0:T(8,128)} %fusion.38, f32[2,8,128,384]{2,3,1,0:T(8,128)} %fusion.40, ...), kind=kOutput, calls=%fused_computation.44 | convolution fusion | flops 510590976 | bytes 35520512 | tf_op jit(solution)/shard_map/bhwc,bcd->bhwd/dot_general | solution.py:46
  (116 shorter events, 47.3 us)
Async XLA Ops:
  6.5 375.3 %copy-start = (bf16[1280,320]{0,1:T(8,128)(2,1)S(1)}, bf16[1280,320]{0,1:T(8,128)(2,1)}, u32[]{:S(2)}) copy-start(bf16[1280,320]{0,1:T(8,128)(2,1)} %param.12) | copy-start | bytes 2457604
  6.5 184.9 %copy-start.5 = (bf16[2,8,128,320]{2,3,1,0:T(8,128)(2,1)S(1)}, bf16[2,8,128,320]{2,3,1,0:T(8,128)(2,1)}, u32[]{:S(2)}) copy-start(bf16[2,8,128,320]{2,3,1,0:T(8,128)(2,1)} %param.10) | copy-start | bytes 3932164
  6.5 309.9 %copy-start.15 = (f32[2,320]{1,0:T(2,128)S(1)}, f32[2,320]{1,0:T(2,128)}, u32[]{:S(2)}) copy-start(f32[2,320]{1,0:T(2,128)} %param.13) | copy-start | bytes 7684
  6.5 309.9 %copy-start.14 = (f32[2,320]{1,0:T(2,128)S(1)}, f32[2,320]{1,0:T(2,128)}, u32[]{:S(2)}) copy-start(f32[2,320]{1,0:T(2,128)} %param.14) | copy-start | bytes 7684
  6.5 397.2 %all-gather.2.cloned.1.call-start = ((), (), s32[]{:S(2)}) async-start(), calls=%async_computation | async-start | bytes 6635520 | tf_op jit(solution)/shard_map/all_gather | solution.py:78
  53.8 266.6 %copy-start.16 = (bf16[1,2,640]{2,1,0:T(2,128)(2,1)S(1)}, bf16[1,2,640]{2,1,0:T(2,128)(2,1)}, u32[]{:S(2)}) copy-start(bf16[1,2,640]{2,1,0:T(2,128)(2,1)} %param.17) | copy-start | bytes 7684
  317.9 64.4 %collective-permute-start = (bf16[2,1,128,320]{2,3,1,0:T(8,128)(2,1)S(1)}, bf16[2,1,128,320]{2,3,1,0:T(8,128)(2,1)S(1)}, u32[]{:S(2)}, u32[]{:S(2)}) collective-permute-start(bf16[2,1,128,320]{2,3,1,0:T(8,128)(2,1)S(1)} %get-tuple-element.23), channel_id=1, source_target_pairs={{0,8},{8,16},{16,24},{24,32},{32,40},{40,48},{48,56},{56,64},{64,7... | collective-permute-start | bytes 491528 | tf_op jit(solution)/shard_map/ppermute | solution.py:14
  319.2 63.1 %collective-permute-start.1 = (bf16[2,1,128,320]{2,3,1,0:T(8,128)(2,1)S(1)}, bf16[2,1,128,320]{2,3,1,0:T(8,128)(2,1)S(1)}, u32[]{:S(2)}, u32[]{:S(2)}) collective-permute-start(bf16[2,1,128,320]{2,3,1,0:T(8,128)(2,1)S(1)} %get-tuple-element.24), channel_id=1, source_target_pairs={{8,0},{16,8},{24,16},{32,24},{40,32},{48,40},{56,48},{64,56},{72,6... | collective-permute-start | bytes 491528 | tf_op jit(solution)/shard_map/ppermute | solution.py:17
  377.0 4.8 copy-start.13
  377.0 5.1 copy-start.17
  377.0 5.1 copy-start.18
  386.9 7.8 collective-permute-start.2
  390.1 6.3 collective-permute-start.3
  419.1 3.4 copy-start.12
  422.5 1.9 copy-start.8
  425.4 2.7 copy-start.7
  442.2 2.7 copy-start.10
  708.7 5.5 copy-start.11
  710.1 9.8 %copy-start.3 = (bf16[2,8,128,320]{2,3,1,0:T(8,128)(2,1)}, bf16[2,8,128,320]{2,3,1,0:T(8,128)(2,1)S(1)}, u32[]{:S(2)}) copy-start(bf16[2,8,128,320]{2,3,1,0:T(8,128)(2,1)S(1)} %multiply_convert_fusion) | copy-start | bytes 3932164
  710.2 7.9 %collective-permute-start.4 = (bf16[2,1,128,320]{2,3,1,0:T(8,128)(2,1)S(1)}, bf16[2,1,128,320]{2,3,1,0:T(8,128)(2,1)S(1)}, u32[]{:S(2)}, u32[]{:S(2)}) collective-permute-start(bf16[2,1,128,320]{2,3,1,0:T(8,128)(2,1)S(1)} %get-tuple-element.21), channel_id=1, source_target_pairs={{0,8},{8,16},{16,24},{24,32},{32,40},{40,48},{48,56},{56,64},{64,7... | collective-permute-start | bytes 491528 | tf_op jit(solution)/shard_map/ppermute | solution.py:14
  712.9 7.0 collective-permute-start.5
  714.8 3.2 copy-start.2
  724.4 13.8 %collective-permute-start.6 = (bf16[2,10,1,320]{3,0,2,1:T(2,128)(2,1)S(1)}, bf16[2,10,1,320]{3,0,2,1:T(2,128)(2,1)S(1)}, u32[]{:S(2)}, u32[]{:S(2)}) collective-permute-start(bf16[2,10,1,320]{3,0,2,1:T(2,128)(2,1)S(1)} %copy.104), channel_id=1, source_target_pairs={{0,1},{2,3},{4,5},{6,7},{8,9},{10,11},{12,13},{14,15},{16,17},{18,... | collective-permute-start | bytes 38408 | tf_op jit(solution)/shard_map/ppermute | solution.py:14
  725.7 9.8 %slice-start = ((s8[4423680]{0:T(1024)(128)(4,1)}), s8[229376]{0:T(1024)(128)(4,1)S(1)}, s32[]{:S(2)}) async-start(s8[4423680]{0:T(1024)(128)(4,1)} %bitcast.145), calls=%async_computation.1 | async-start | bytes 458752
  727.7 7.8 %slice-start.1 = ((s8[4423680]{0:T(1024)(128)(4,1)}), s8[4194304]{0:T(1024)(128)(4,1)S(1)}, s32[]{:S(2)}) async-start(s8[4423680]{0:T(1024)(128)(4,1)} %bitcast.145), calls=%async_computation.2 | async-start | bytes 8388608
  727.7 7.8 %copy-start.4 = (bf16[2,8,128,320]{2,3,1,0:T(8,128)(2,1)S(1)}, bf16[2,8,128,320]{2,3,1,0:T(8,128)(2,1)}, u32[]{:S(2)}) copy-start(bf16[2,8,128,320]{2,3,1,0:T(8,128)(2,1)} %copy-done.3) | copy-start | bytes 3932164
  727.7 12.5 %collective-permute-start.7 = (bf16[2,10,1,320]{3,0,2,1:T(2,128)(2,1)S(1)}, bf16[2,10,1,320]{3,0,2,1:T(2,128)(2,1)S(1)}, u32[]{:S(2)}, u32[]{:S(2)}) collective-permute-start(bf16[2,10,1,320]{3,0,2,1:T(2,128)(2,1)S(1)} %copy.109), channel_id=1, source_target_pairs={{1,0},{3,2},{5,4},{7,6},{9,8},{11,10},{13,12},{15,14},{17,16},{19,... | collective-permute-start | bytes 38408 | tf_op jit(solution)/shard_map/ppermute | solution.py:17
  740.1 6.7 slice-start.2
  741.8 5.0 slice-start.3
  758.0 2.7 copy-start.9
  760.7 8.9 %copy-start.6 = (bf16[2,8,128,320]{2,3,1,0:T(8,128)(2,1)S(1)}, bf16[2,8,128,320]{2,3,1,0:T(8,128)(2,1)}, u32[]{:S(2)}) copy-start(bf16[2,8,128,320]{2,3,1,0:T(8,128)(2,1)} %param.10) | copy-start | bytes 3932164
  760.7 10.6 %copy-start.1 = (bf16[1280,320]{0,1:T(8,128)(2,1)S(1)}, bf16[1280,320]{0,1:T(8,128)(2,1)}, u32[]{:S(2)}) copy-start(bf16[1280,320]{0,1:T(8,128)(2,1)} %param.12) | copy-start | bytes 2457604
Sparse Core Ops, SparseCore 0:
  54.0 51.1 all-gather.1
where the time goes:
time: 784 us; the launch traced here: 778 us
  blocking collectives  614 us (78%)
  matrix products  79 us (10%)
  local copies, waits for them, and re-layouts  37.7 us (5%)
  other arithmetic  17 us (2%)
  starting transfers between devices  15 us (2%)
  between operations  14.1 us (2%)
    psum x2, blocking collectives, group_act(): total = lax.psum(jnp.sum(grouped, axis=(1, 2, 4)), ('patch', 'owner'))  258 us
    psum x2, blocking collectives, group_act(): lax.psum(jnp.sum(centered * centered, axis=(1, 2, 4)), ('patch', 'owner'))  252 us
    dot_general x18, matrix products, block_conv(): jnp.einsum('bhwc,bcd->bhwd', window, joined[:, tap], preferred_element_ty...  62.9 us
    all_gather x1, blocking collectives, local(): lax.all_gather(plugin_reduce_library, 'patch', axis=2, tiled=True)  47.2 us
    all_gather x1, blocking collectives, local(): lax.all_gather(plugin_expand_library, 'patch', axis=2, tiled=True)  32 us
    all_gather x1, blocking collectives, local(): lax.all_gather(full_up, ('req', 'owner'), axis=0, tiled=True)  24.4 us
  transfers between devices with their start and end apart: 9, of which 1 were waited for; matrix products, arithmetic and copies ran while one was open for 5% of the time, Pallas kernels for 0%

commit v1 on v0

--- a/solution.py
+++ b/solution.py
@@ -26,7 +26,7 @@
     total = lax.psum(jnp.sum(grouped, axis=(1, 2, 4)), ("patch", "owner"))
     mean = total / count
     centered = grouped - mean[:, None, None, :, None]
-    spread = lax.psum(jnp.sum(centered * centered, axis=(1, 2, 4)), ("patch", "owner"))
+    spread = lax.psum(lax.psum(jnp.sum(centered * centered, axis=(1, 2, 4)), "owner"), "patch")
     var = spread / count
     normed = (centered / jnp.sqrt(var + 1e-05)[:, None, None, :, None]).reshape(values.shape)
     return jax.nn.silu(normed * gain + shift).astype(jnp.bfloat16)

time: 784 us -> 685 us (0.87)
  blocking collectives: 614 us -> 497 us
  starting transfers between devices: 15 us -> 33.1 us
    psum x2 -> x4, blocking collectives: 252 us -> 121 us  [the longest x2 112 us: group_act(): lax.psum(lax.psum(jnp.sum(centered * centered, axis=(1, 2, 4)), 'owner'),...]
    all_gather x1, blocking collectives: 24.4 us -> 38.2 us  [local(): lax.all_gather(full_up, ('req', 'owner'), axis=0, tiled=True)]
    ppermute x4, starting transfers between devices: 9.78 us -> 23.5 us  [padded_2(): lax.ppermute(lax.slice_in_dim(block, 0, width, axis=dim), axis, backward)]
  transfers between devices with their start and end apart: 9 -> 9, of which waited for: 1 -> 1; matrix products, arithmetic and copies ran while one was open for 5% -> 6% of each run, Pallas kernels for 0% -> 0%
where the time goes in v1:
time: 685 us; the launch traced here: 679 us
  blocking collectives  497 us (73%)
  matrix products  79 us (12%)
  local copies, waits for them, and re-layouts  37.7 us (6%)
  starting transfers between devices  33.1 us (5%)
  other arithmetic  17 us (2%)
  between operations  14.1 us (2%)
    psum x2, blocking collectives, group_act(): total = lax.psum(jnp.sum(grouped, axis=(1, 2, 4)), ('patch', 'owner'))  258 us
    psum x2, blocking collectives, group_act(): lax.psum(lax.psum(jnp.sum(centered * centered, axis=(1, 2, 4)), 'owner'),...  112 us
    dot_general x18, matrix products, block_conv(): jnp.einsum('bhwc,bcd->bhwd', window, joined[:, tap], preferred_element_ty...  62.9 us
    all_gather x1, blocking collectives, local(): lax.all_gather(plugin_reduce_library, 'patch', axis=2, tiled=True)  47.2 us
    all_gather x1, blocking collectives, local(): lax.all_gather(full_up, ('req', 'owner'), axis=0, tiled=True)  38.2 us
    all_gather x1, blocking collectives, local(): lax.all_gather(plugin_expand_library, 'patch', axis=2, tiled=True)  32 us
    ppermute x4, starting transfers between devices, padded_2(): lax.ppermute(lax.slice_in_dim(block, 0, width, axis=dim), axis, backward)  23.5 us
  transfers between devices with their start and end apart: 9, of which 1 were waited for; matrix products, arithmetic and copies ran while one was open for 6% of the time, Pallas kernels for 0%

profile of v1, /device:TPU:1, one launch (start us, length us, event | category | flops | bytes accessed | tf_op | source)
XLA Modules:
  0.0 679.0 jit_solution(7872060228628531882)
XLA Ops:
  6.6 47.2 %all_gather.12 = bf16[1,2,184320]{2,1,0:T(2,128)(2,1)} all-gather(bf16[1,2,5760]{2,1,0:T(2,128)(2,1)} %param.16), channel_id=1, replica_groups=mesh['patch'=32,'req'=4,'owner'=2] {'patch'}, dimensions={2}, use_global_device_ids=true | all-gather | bytes 760320 | tf_op jit(solution)/shard_map/all_gather | solution.py:74
  55.6 135.6 %psum.42 = f32[2,32]{1,0:T(2,128)S(1)} all-reduce(f32[2,32]{1,0:T(2,128)S(1)} %reduce_sum.59), channel_id=1, replica_groups=mesh['patch'=32,'req'=4,'owner'=2] {'patch','owner'}, use_global_device_ids=true, to_apply=%region_2.3 | all-reduce | flops 64 | bytes 512 | tf_op jit(solution)/shard_map/psum | solution.py:26
  192.2 2.8 psum.43
  194.9 56.0 %psum.44 = f32[2,32]{1,0:T(2,128)S(1)} all-reduce(f32[2,32]{1,0:T(2,128)S(1)} %psum.43), channel_id=1, replica_groups=mesh['patch'=32,'req'=4,'owner'=2] {'patch'}, use_global_device_ids=true, to_apply=%region_6.7 | all-reduce | flops 64 | bytes 512 | tf_op jit(solution)/shard_map/psum | solution.py:29
  252.6 3.5 collective-permute-start
  257.4 32.0 %all_gather.14 = bf16[1,2,20480]{2,1,0:T(2,128)(2,1)S(1)} all-gather(bf16[1,2,640]{2,1,0:T(2,128)(2,1)S(1)} %copy-done.16), channel_id=1, replica_groups=mesh['patch'=32,'req'=4,'owner'=2] {'patch'}, dimensions={2}, use_global_device_ids=true | all-gather | bytes 84480 | tf_op jit(solution)/shard_map/all_gather | solution.py:75
  289.4 38.2 %all_gather.15 = bf16[8,2,20480]{2,1,0:T(2,128)(2,1)S(1)} all-gather(bf16[1,2,20480]{2,1,0:T(2,128)(2,1)S(1)} %all_gather.14), channel_id=1, replica_groups=mesh['patch'=32,'req'=4,'owner'=2] {'req','owner'}, dimensions={0}, use_global_device_ids=true | all-gather | bytes 737280 | tf_op jit(solution)/shard_map/all_gather | solution.py:79
  327.6 4.8 slice_bitcast_fusion
  340.7 3.5 collective-permute-start.3
  348.6 5.7 pad_maximum_fusion
  354.4 10.7 %convolution_convert_fusion = bf16[2,2,184320]{2,0,1:T(2,128)(2,1)} fusion(bf16[8,2,184320]{2,1,0:T(2,128)(2,1)} %all-gather.2.cloned.1.call-done, s32[2]{0:T(128)S(1)} %fusion.123), kind=kOutput, calls=%fused_computation | convolution fusion | flops 12533776 | bytes 7372808 | tf_op jit(solution)/shard_map/ik,kjs->ijs/dot_general | solution.py:83
  365.1 4.7 reshape.54
  369.7 3.3 fusion.145
  376.1 2.7 fusion.52
  378.8 2.9 fusion.54
  381.7 2.9 fusion.50
  384.6 2.7 fusion.48
  390.1 2.7 fusion.14
  392.8 2.7 fusion.18
  395.5 9.6 %add_add_fusion.1 = f32[2,8,128,384]{2,3,1,0:T(8,128)} fusion(f32[2,8,128,384]{2,3,1,0:T(8,128)} %fusion.18, f32[2,8,128,384]{2,3,1,0:T(8,128)} %fusion.48, f32[2,8,128,384]{2,3,1,0:T(8,128)} %fusion.50, f32[2,8,128,384]{2,3,1,0:T(8,128)} %fusion.80, f32[2,8,128,384]{2,3,1,0:T(8,128)S(1)} %copy-done.10, f32[2,8,128,384]{2,3,1,0:T(8,128)} %fusion.54, ...), kind=kOutput, calls=%fused_computation.45 | convolution fusion | flops 510590976 | bytes 35520512 | tf_op jit(solution)/shard_map/bhwc,bcd->bhwd/dot_general | solution.py:46
  408.0 122.8 %psum.45 = f32[2,32]{1,0:T(2,128)S(1)} all-reduce(f32[2,32]{1,0:T(2,128)S(1)} %reduce_sum.82), channel_id=1, replica_groups=mesh['patch'=32,'req'=4,'owner'=2] {'patch','owner'}, use_global_device_ids=true, to_apply=%region_10.11 | all-reduce | flops 64 | bytes 512 | tf_op jit(solution)/shard_map/psum | solution.py:26
  531.7 6.0 psum.46
  537.7 56.2 %psum.47 = f32[2,32]{1,0:T(2,128)S(1)} all-reduce(f32[2,32]{1,0:T(2,128)S(1)} %psum.46), channel_id=1, replica_groups=mesh['patch'=32,'req'=4,'owner'=2] {'patch'}, use_global_device_ids=true, to_apply=%region_14.15 | all-reduce | flops 64 | bytes 512 | tf_op jit(solution)/shard_map/psum | solution.py:29
  595.5 3.5 collective-permute-start.4
  602.4 3.2 fusion.97
  614.6 17.4 %collective-permute-start.7 = (bf16[2,10,1,320]{3,0,2,1:T(2,128)(2,1)S(1)}, bf16[2,10,1,320]{3,0,2,1:T(2,128)(2,1)S(1)}, u32[]{:S(2)}, u32[]{:S(2)}) collective-permute-start(bf16[2,10,1,320]{3,0,2,1:T(2,128)(2,1)S(1)} %copy.109), channel_id=1, source_target_pairs={{1,0},{3,2},{5,4},{7,6},{9,8},{11,10},{13,12},{15,14},{17,16},{19,... | collective-permute-start | bytes 38408 | tf_op jit(solution)/shard_map/ppermute | solution.py:17
  632.0 4.1 fusion.22
  636.1 2.7 fusion.26
  642.4 5.0 pad_maximum_fusion.1
  652.8 2.9 fusion.40
  655.7 2.9 fusion.36
  661.3 8.9 %add_add_fusion = f32[2,8,128,384]{2,3,1,0:T(8,128)S(1)} fusion(f32[2,8,128,384]{2,3,1,0:T(8,128)} %fusion.26, f32[2,8,128,384]{2,3,1,0:T(8,128)} %fusion.34, f32[2,8,128,384]{2,3,1,0:T(8,128)} %fusion.36, f32[2,8,128,384]{2,3,1,0:T(8,128)S(1)} %copy-done.9, f32[2,8,128,384]{2,3,1,0:T(8,128)} %fusion.38, f32[2,8,128,384]{2,3,1,0:T(8,128)} %fusion.40, ...), kind=kOutput, calls=%fused_computation.44 | convolution fusion | flops 510590976 | bytes 35520512 | tf_op jit(solution)/shard_map/bhwc,bcd->bhwd/dot_general | solution.py:46
  (118 shorter events, 54.8 us)
Async XLA Ops:
  6.5 325.9 %copy-start = (bf16[1280,320]{0,1:T(8,128)(2,1)S(1)}, bf16[1280,320]{0,1:T(8,128)(2,1)}, u32[]{:S(2)}) copy-start(bf16[1280,320]{0,1:T(8,128)(2,1)} %param.12) | copy-start | bytes 2457604
  6.5 184.9 %copy-start.5 = (bf16[2,8,128,320]{2,3,1,0:T(8,128)(2,1)S(1)}, bf16[2,8,128,320]{2,3,1,0:T(8,128)(2,1)}, u32[]{:S(2)}) copy-start(bf16[2,8,128,320]{2,3,1,0:T(8,128)(2,1)} %param.10) | copy-start | bytes 3932164
  6.5 244.6 %copy-start.15 = (f32[2,320]{1,0:T(2,128)S(1)}, f32[2,320]{1,0:T(2,128)}, u32[]{:S(2)}) copy-start(f32[2,320]{1,0:T(2,128)} %param.13) | copy-start | bytes 7684
  6.5 244.6 %copy-start.14 = (f32[2,320]{1,0:T(2,128)S(1)}, f32[2,320]{1,0:T(2,128)}, u32[]{:S(2)}) copy-start(f32[2,320]{1,0:T(2,128)} %param.14) | copy-start | bytes 7684
  6.5 347.8 %all-gather.2.cloned.1.call-start = ((), (), s32[]{:S(2)}) async-start(), calls=%async_computation | async-start | bytes 6635520 | tf_op jit(solution)/shard_map/all_gather | solution.py:78
  53.8 203.5 %copy-start.16 = (bf16[1,2,640]{2,1,0:T(2,128)(2,1)S(1)}, bf16[1,2,640]{2,1,0:T(2,128)(2,1)}, u32[]{:S(2)}) copy-start(bf16[1,2,640]{2,1,0:T(2,128)(2,1)} %param.17) | copy-start | bytes 7684
  252.6 80.4 %collective-permute-start = (bf16[2,1,128,320]{2,3,1,0:T(8,128)(2,1)S(1)}, bf16[2,1,128,320]{2,3,1,0:T(8,128)(2,1)S(1)}, u32[]{:S(2)}, u32[]{:S(2)}) collective-permute-start(bf16[2,1,128,320]{2,3,1,0:T(8,128)(2,1)S(1)} %get-tuple-element.23), channel_id=1, source_target_pairs={{0,8},{8,16},{16,24},{24,32},{32,40},{40,48},{48,56},{56,64},{64,7... | collective-permute-start | bytes 491528 | tf_op jit(solution)/shard_map/ppermute | solution.py:14
  256.1 76.9 %collective-permute-start.1 = (bf16[2,1,128,320]{2,3,1,0:T(8,128)(2,1)S(1)}, bf16[2,1,128,320]{2,3,1,0:T(8,128)(2,1)S(1)}, u32[]{:S(2)}, u32[]{:S(2)}) collective-permute-start(bf16[2,1,128,320]{2,3,1,0:T(8,128)(2,1)S(1)} %get-tuple-element.24), channel_id=1, source_target_pairs={{8,0},{16,8},{24,16},{32,24},{40,32},{48,40},{56,48},{64,56},{72,6... | collective-permute-start | bytes 491528 | tf_op jit(solution)/shard_map/ppermute | solution.py:17
  327.6 4.8 copy-start.13
  327.6 5.1 copy-start.17
  327.6 5.1 copy-start.18
  337.5 7.8 %collective-permute-start.2 = (bf16[2,10,1,320]{3,0,2,1:T(2,128)(2,1)S(1)}, bf16[2,10,1,320]{3,0,2,1:T(2,128)(2,1)S(1)}, u32[]{:S(2)}, u32[]{:S(2)}) collective-permute-start(bf16[2,10,1,320]{3,0,2,1:T(2,128)(2,1)S(1)} %copy.87), channel_id=1, source_target_pairs={{0,1},{2,3},{4,5},{6,7},{8,9},{10,11},{12,13},{14,15},{16,17},{18,... | collective-permute-start | bytes 38408 | tf_op jit(solution)/shard_map/ppermute | solution.py:14
  340.7 6.3 collective-permute-start.3
  369.7 3.4 copy-start.12
  373.1 1.9 copy-start.8
  376.1 2.7 copy-start.7
  392.8 2.7 copy-start.10
  594.0 7.7 %copy-start.11 = (bf16[9,320,320]{2,1,0:T(8,128)(2,1)S(1)}, bf16[9,320,320]{2,1,0:T(8,128)(2,1)}, u32[]{:S(2)}) copy-start(bf16[9,320,320]{2,1,0:T(8,128)(2,1)} %get-tuple-element.9) | copy-start | bytes 5529604
  595.4 11.4 %copy-start.3 = (bf16[2,8,128,320]{2,3,1,0:T(8,128)(2,1)}, bf16[2,8,128,320]{2,3,1,0:T(8,128)(2,1)S(1)}, u32[]{:S(2)}) copy-start(bf16[2,8,128,320]{2,3,1,0:T(8,128)(2,1)S(1)} %multiply_convert_fusion) | copy-start | bytes 3932164
  595.5 10.1 %collective-permute-start.4 = (bf16[2,1,128,320]{2,3,1,0:T(8,128)(2,1)S(1)}, bf16[2,1,128,320]{2,3,1,0:T(8,128)(2,1)S(1)}, u32[]{:S(2)}, u32[]{:S(2)}) collective-permute-start(bf16[2,1,128,320]{2,3,1,0:T(8,128)(2,1)S(1)} %get-tuple-element.21), channel_id=1, source_target_pairs={{0,8},{8,16},{16,24},{24,32},{32,40},{40,48},{48,56},{56,64},{64,7... | collective-permute-start | bytes 491528 | tf_op jit(solution)/shard_map/ppermute | solution.py:14
  600.4 6.4 collective-permute-start.5
  602.3 3.2 copy-start.2
  611.3 27.6 %collective-permute-start.6 = (bf16[2,10,1,320]{3,0,2,1:T(2,128)(2,1)S(1)}, bf16[2,10,1,320]{3,0,2,1:T(2,128)(2,1)S(1)}, u32[]{:S(2)}, u32[]{:S(2)}) collective-permute-start(bf16[2,10,1,320]{3,0,2,1:T(2,128)(2,1)S(1)} %copy.104), channel_id=1, source_target_pairs={{0,1},{2,3},{4,5},{6,7},{8,9},{10,11},{12,13},{14,15},{16,17},{18,... | collective-permute-start | bytes 38408 | tf_op jit(solution)/shard_map/ppermute | solution.py:14
  612.6 23.5 %slice-start = ((s8[4423680]{0:T(1024)(128)(4,1)}), s8[229376]{0:T(1024)(128)(4,1)S(1)}, s32[]{:S(2)}) async-start(s8[4423680]{0:T(1024)(128)(4,1)} %bitcast.145), calls=%async_computation.1 | async-start | bytes 458752
  614.5 21.6 %slice-start.1 = ((s8[4423680]{0:T(1024)(128)(4,1)}), s8[4194304]{0:T(1024)(128)(4,1)S(1)}, s32[]{:S(2)}) async-start(s8[4423680]{0:T(1024)(128)(4,1)} %bitcast.145), calls=%async_computation.2 | async-start | bytes 8388608
  614.5 21.6 %copy-start.4 = (bf16[2,8,128,320]{2,3,1,0:T(8,128)(2,1)S(1)}, bf16[2,8,128,320]{2,3,1,0:T(8,128)(2,1)}, u32[]{:S(2)}) copy-start(bf16[2,8,128,320]{2,3,1,0:T(8,128)(2,1)} %copy-done.3) | copy-start | bytes 3932164
  614.6 26.2 %collective-permute-start.7 = (bf16[2,10,1,320]{3,0,2,1:T(2,128)(2,1)S(1)}, bf16[2,10,1,320]{3,0,2,1:T(2,128)(2,1)S(1)}, u32[]{:S(2)}, u32[]{:S(2)}) collective-permute-start(bf16[2,10,1,320]{3,0,2,1:T(2,128)(2,1)S(1)} %copy.109), channel_id=1, source_target_pairs={{1,0},{3,2},{5,4},{7,6},{9,8},{11,10},{13,12},{15,14},{17,16},{19,... | collective-permute-start | bytes 38408 | tf_op jit(solution)/shard_map/ppermute | solution.py:17
  640.7 6.7 slice-start.2
  642.4 5.0 slice-start.3
  658.6 2.7 copy-start.9
  661.3 8.9 %copy-start.6 = (bf16[2,8,128,320]{2,3,1,0:T(8,128)(2,1)S(1)}, bf16[2,8,128,320]{2,3,1,0:T(8,128)(2,1)}, u32[]{:S(2)}) copy-start(bf16[2,8,128,320]{2,3,1,0:T(8,128)(2,1)} %param.10) | copy-start | bytes 3932164
  661.3 10.6 %copy-start.1 = (bf16[1280,320]{0,1:T(8,128)(2,1)S(1)}, bf16[1280,320]{0,1:T(8,128)(2,1)}, u32[]{:S(2)}) copy-start(bf16[1280,320]{0,1:T(8,128)(2,1)} %param.12) | copy-start | bytes 2457604
Sparse Core Ops, SparseCore 0:
  54.0 51.1 all-gather.1
